TPU v7x, 32 devices: a whole 2x2x4 slice. The times are simulated.
32 devices in a mesh: section: 4 (over y, core), expert: 8 (over z, x).
Axes of the slice: x: 2, y: 2, z: 4, core: 2. Of those that a mesh axis runs over, the one named last changes fastest.
Arguments:
- states: bfloat16 [4, 64, 3584], P('section', 'expert'), may hold values from -6 to 6
- norm_gain: float32 [4, 3584], P('section'), may hold values from 0.1 to 1.9
- router: bfloat16 [4, 3584, 4], P('section'), may hold values from -0.09375 to 0.09375
- w_gate: bfloat16 [4, 3584, 4096], P('section', None, 'expert'), may hold values from -0.09375 to 0.09375
- w_up: bfloat16 [4, 3584, 4096], P('section', None, 'expert'), may hold values from -0.09375 to 0.09375
- w_down: bfloat16 [4, 4096, 3584], P('section', 'expert'), may hold values from -0.1875 to 0.1875
- routes: int32 [2, 4, 64, 2], P(None, 'section', 'expert'), may hold values from 0 to 3, all different within a row; in each aligned block of 8 rows (0 to 7, 8 to 15, ..., all dimensions but the last counted through in order) at most 8 rows name the same one
Outputs:
- final_states: bfloat16 [4, 64, 3584], P('section', 'expert')
Inputs may be any that keep to these rules, and one draw needn't show every extreme that they name: `routes`: each token names 2 different experts. Within one tick and one section, among the 8 tokens of one index of the expert axis, no expert is named by more than 8 tokens; in some such blocks one expert is named by exactly 8.
All inputs are finite; a program needn't handle non-finite values.
Results may differ from a plain program's by a relative error of at most 0.0064.
Values may be sent and summed in bfloat16 or wider, within the bound.
No kernel may reach another device: no remote copies, remote signals or barrier semaphores. Data moves between devices by JAX's collectives and lax.ppermute only.
A program may use at most 64 MiB of HBM per device.

v0:
```python
import functools

import jax
import jax.numpy as jnp
from jax import lax
from jax.experimental import pallas as pl
from jax.experimental.pallas import tpu as pltpu
from jax.sharding import PartitionSpec as P


TICKS = 2
EPSILON = 1e-06
AXES = ("section", "expert")
LANES = 128
PIECES = 3
FETCHES = 4
VMEM_BYTES = 64 << 20


def relayed(value, sections, experts, shards, hop, expert_bits, shard_bits):
    devices = experts * shards
    pairs = []
    for s in range(sections):
        for e in range(experts):
            for h in range(shards):
                target = (e ^ expert_bits) * shards + (h ^ shard_bits)
                pairs.append((s * devices + e * shards + h, (s + hop) % sections * devices + target))
    return lax.ppermute(value, AXES, pairs)


def fetch_kernel(count, *refs):
    copies = []
    for i in range(count):
        source, target = refs[i], refs[count + i]
        step = source.shape[0] // FETCHES
        for part in range(FETCHES):
            span = pl.ds(part * step, step)
            copies.append(
                pltpu.make_async_copy(source.at[span], target.at[span], refs[2 * count].at[i * FETCHES + part])
            )
    for copy in copies:
        copy.start()
    for copy in copies:
        copy.wait()


def fetched(*weights):
    count = len(weights)
    held = sum(w.size * w.dtype.itemsize for w in weights)
    return pl.pallas_call(
        functools.partial(fetch_kernel, count),
        out_shape=tuple(pltpu.VMEM(w.shape, w.dtype) for w in weights),
        in_specs=[pl.BlockSpec(memory_space=pl.ANY)] * count,
        out_specs=[pl.BlockSpec(memory_space=pltpu.VMEM)] * count,
        scratch_shapes=[pltpu.SemaphoreType.DMA((count * FETCHES,))],
        compiler_params=pltpu.CompilerParams(vmem_limit_bytes=VMEM_BYTES - held - held // 5),
    )(*weights)


def share_kernel(own_ref, ids_ref, home_ref, gain_ref, router_ref, out_ref):
    rows, width = own_ref.shape
    experts = router_ref.shape[0]
    values = own_ref[...].astype(jnp.float32)
    meansq = jnp.mean(values * values, axis=-1, keepdims=True)
    normed = (values * lax.rsqrt(meansq + EPSILON) * gain_ref[...]).astype(jnp.bfloat16)
    logits = lax.dot_general(
        normed, router_ref[...], (((1,), (1,)), ((), ())), preferred_element_type=jnp.float32
    )
    affinity = jax.nn.sigmoid(logits)
    column = lax.broadcasted_iota(jnp.int32, (rows, experts), 1)
    named = jnp.zeros((rows, experts), jnp.bool_)
    for k in range(ids_ref.shape[1]):
        named = named | (ids_ref[:, k : k + 1] == column)
    chosen = jnp.where(named, affinity, 0.0)
    gates = chosen / jnp.sum(chosen, axis=1, keepdims=True)
    lane = lax.broadcasted_iota(jnp.int32, (rows, LANES), 1)
    extra = jnp.zeros((rows, LANES), jnp.float32)
    for k in range(experts):
        rest = jnp.sum(jnp.where(column == (home_ref[0] ^ k), gates, 0.0), axis=1, keepdims=True)
        for piece in range(PIECES):
            top = rest.astype(jnp.bfloat16).astype(jnp.float32)
            extra = jnp.where(lane == k * PIECES + piece, top, extra)
            rest = rest - top
    out_ref[:, :width] = own_ref[...]
    out_ref[:, width:] = extra.astype(jnp.bfloat16)


def with_shares(own, expert_ids, home, gain, router):
    rows, width = own.shape
    vmem = pl.BlockSpec(memory_space=pltpu.VMEM)
    return pl.pallas_call(
        share_kernel,
        out_shape=jax.ShapeDtypeStruct((rows, width + LANES), jnp.bfloat16),
        in_specs=[vmem, vmem, pl.BlockSpec(memory_space=pltpu.SMEM), vmem, vmem],
        out_specs=vmem,
        compiler_params=pltpu.CompilerParams(vmem_limit_bytes=4 << 20),
        name="shares",
    )(own, expert_ids, home, gain, router)


def fold_kernel(shards, *refs):
    outs = refs[shards:]
    rows = outs[0].shape[0]
    for k, out in enumerate(outs):
        span = pl.ds(k * rows, rows)
        total = refs[0][span, :].astype(jnp.float32)
        for part in refs[1:shards]:
            total = total + part[span, :].astype(jnp.float32)
        out[...] = total.astype(out.dtype)


def folded(parts, experts):
    rows, width = parts[0].shape[0] // experts, parts[0].shape[1]
    vmem = pl.BlockSpec(memory_space=pltpu.VMEM)
    return pl.pallas_call(
        functools.partial(fold_kernel, len(parts)),
        out_shape=tuple(
            jax.ShapeDtypeStruct((rows, width), jnp.float32 if k == 0 else jnp.bfloat16) for k in range(experts)
        ),
        in_specs=[vmem] * len(parts),
        out_specs=[vmem] * experts,
        compiler_params=pltpu.CompilerParams(vmem_limit_bytes=4 << 20),
        name="fold",
    )(*parts)


def finish_kernel(count, shared_ref, *refs):
    out_ref = refs[count]
    width = out_ref.shape[1]
    total = shared_ref[:, :width].astype(jnp.float32)
    extra = shared_ref[:, width:].astype(jnp.float32)
    lane = lax.broadcasted_iota(jnp.int32, extra.shape, 1)
    for k in range(count):
        terms = jnp.where((lane >= k * PIECES) & (lane < (k + 1) * PIECES), extra, 0.0)
        total = total + jnp.sum(terms, axis=1, keepdims=True) * refs[k][...].astype(jnp.float32)
    out_ref[...] = total.astype(jnp.bfloat16)


def finished(shared, pieces):
    rows, width = pieces[0].shape
    vmem = pl.BlockSpec(memory_space=pltpu.VMEM)
    return pl.pallas_call(
        functools.partial(finish_kernel, len(pieces)),
        out_shape=jax.ShapeDtypeStruct((rows, width), jnp.bfloat16),
        in_specs=[vmem] * (1 + len(pieces)),
        out_specs=vmem,
        compiler_params=pltpu.CompilerParams(vmem_limit_bytes=4 << 20),
        name="finish",
    )(shared, *pieces)


def expert_kernel(count, shards, *refs):
    blocks = refs[:count]
    gain_ref, gate_ref, lift_ref, down_ref = refs[count : count + 4]
    outs = refs[count + 4 : count + 4 + shards]
    normed_ref = refs[count + 4 + shards]
    rows = blocks[0].shape[0]
    gain = gain_ref[...]
    for pair in range(0, count, 2):
        parts = []
        for block in blocks[pair : pair + 2]:
            values = block[...].astype(jnp.float32)
            meansq = jnp.mean(values * values, axis=-1, keepdims=True)
            parts.append(values * lax.rsqrt(meansq + EPSILON) * gain)
        normed_ref[pl.ds(pair * rows, 2 * rows), :] = jnp.concatenate(parts, axis=0).astype(jnp.bfloat16)
    normed = normed_ref[...]
    gate_out = jnp.dot(normed, gate_ref[...], preferred_element_type=jnp.float32)
    lifted = jnp.dot(normed, lift_ref[...], preferred_element_type=jnp.float32)
    hidden = (gate_out / (1.0 + jnp.exp(-gate_out)) * lifted).astype(jnp.bfloat16)
    partial_value = jnp.dot(hidden, down_ref[...], preferred_element_type=jnp.float32).astype(jnp.bfloat16)
    share = partial_value.shape[0] // shards
    for i, out in enumerate(outs):
        out[...] = partial_value[i * share : (i + 1) * share]


def expert_parts(blocks, gain, gate, lift, down, shards):
    count = len(blocks)
    rows, width = blocks[0].shape
    return pl.pallas_call(
        functools.partial(expert_kernel, count, shards),
        out_shape=tuple(
            jax.ShapeDtypeStruct((count // shards * rows, width), jnp.bfloat16) for _ in range(shards)
        ),
        in_specs=[pl.BlockSpec(memory_space=pltpu.VMEM)] * (count + 4),
        out_specs=[pl.BlockSpec(memory_space=pltpu.VMEM)] * shards,
        scratch_shapes=[pltpu.VMEM((count * rows, width), jnp.bfloat16)],
        compiler_params=pltpu.CompilerParams(vmem_limit_bytes=8 << 20),
        name="experts",
    )(*blocks, gain, gate, lift, down)


def on_device(states, norm_gain, router, w_gate, w_up, w_down, routes):
    sections = lax.axis_size("section")
    devices = lax.axis_size("expert")
    experts = router.shape[2]
    shards = devices // experts
    send = functools.partial(relayed, sections=sections, experts=experts, shards=shards)
    far_first = range(experts - 1, 0, -1)

    def gathered(own):
        line = {0: own}
        for k in far_first:
            line[k] = send(own, hop=0, expert_bits=k, shard_bits=0)
        blocks = {(0, k): line[k] for k in range(experts)}
        for k in range(experts):
            for j in range(1, shards):
                blocks[j, k] = send(line[k], hop=0, expert_bits=0, shard_bits=j)
        return [blocks[j, k] for j in range(shards) for k in range(experts)]

    current = states[0]
    home = (lax.axis_index("expert") // shards).astype(jnp.int32)[None]
    for tick in range(TICKS):
        blocks = gathered(current)
        weights = fetched(w_gate[0], w_up[0], w_down[0])
        shared = with_shares(current, routes[tick, 0], home, norm_gain, router[0].T)
        shared = send(shared, hop=1, expert_bits=0, shard_bits=0)
        parts = expert_parts(blocks, norm_gain, *weights, shards)
        sums = folded([send(part, hop=1, expert_bits=0, shard_bits=j) for j, part in enumerate(parts)], experts)
        pieces = {0: sums[0]}
        for k in far_first:
            pieces[k] = send(sums[k], hop=0, expert_bits=k, shard_bits=0)
        current = finished(shared, [pieces[k] for k in range(experts)])
    return current[None]


def solution(mesh):
    placed = (
        P("section", "expert", None),
        P("section", None),
        P("section", None, None),
        P("section", None, "expert"),
        P("section", None, "expert"),
        P("section", "expert", None),
        P(None, "section", "expert", None),
    )
    return jax.shard_map(
        on_device,
        mesh=mesh,
        in_specs=placed,
        out_specs=P("section", "expert", None),
        check_vma=False,
    )
```

profile of v0, /device:TPU:0, one launch (start us, length us, event | category | flops | bytes accessed | tf_op | source)
XLA Modules:
  0.0 78.5 jit_solution(4136103742786204708)
XLA Ops:
  0.0 3.1 %collective-permute-start.1 = (bf16[8,3584]{1,0:T(8,128)(2,1)}, bf16[8,3584]{1,0:T(8,128)(2,1)S(1)}, u32[]{:S(2)}, u32[]{:S(2)}) collective-permute-start(bf16[8,3584]{1,0:T(8,128)(2,1)} %bitcast.13), channel_id=1, source_target_pairs={{0,2},{1,3},{2,0},{3,1},{4,6},{5,7},{6,4},{7,5},{8,10},{9,11},{10,... | collective-permute-start | bytes 172040 | tf_op jit(solution)/shard_map/ppermute | solution.py:28
  3.1 2.6 %collective-permute-start.2 = (bf16[8,3584]{1,0:T(8,128)(2,1)}, bf16[8,3584]{1,0:T(8,128)(2,1)S(1)}, u32[]{:S(2)}, u32[]{:S(2)}) collective-permute-start(bf16[8,3584]{1,0:T(8,128)(2,1)} %bitcast.14), channel_id=1, source_target_pairs={{0,4},{1,5},{2,6},{3,7},{4,0},{5,1},{6,2},{7,3},{8,12},{9,13},{10,... | collective-permute-start | bytes 172040 | tf_op jit(solution)/shard_map/ppermute | solution.py:28
  5.6 1.7 %collective-permute-start.4 = (bf16[8,3584]{1,0:T(8,128)(2,1)}, bf16[8,3584]{1,0:T(8,128)(2,1)S(1)}, u32[]{:S(2)}, u32[]{:S(2)}) collective-permute-start(bf16[8,3584]{1,0:T(8,128)(2,1)} %bitcast.16), channel_id=1, source_target_pairs={{0,1},{1,0},{2,3},{3,2},{4,5},{5,4},{6,7},{7,6},{8,9},{9,8},{10,11... | collective-permute-start | bytes 172040 | tf_op jit(solution)/shard_map/ppermute | solution.py:28
  7.7 1.8 %collective-permute-done.2.refs_2_ = bf16[8,3584]{1,0:T(8,128)(2,1)S(1)} collective-permute-done((bf16[8,3584]{1,0:T(8,128)(2,1)}, bf16[8,3584]{1,0:T(8,128)(2,1)S(1)}, u32[]{:S(2)}, u32[]{:S(2)}) %collective-permute-start.2) | collective-permute-done | bytes 57376 | tf_op jit(solution)/shard_map/ppermute | solution.py:28
  9.5 1.5 %collective-permute-start.6 = (bf16[8,3584]{1,0:T(8,128)(2,1)S(1)}, bf16[8,3584]{1,0:T(8,128)(2,1)S(1)}, u32[]{:S(2)}, u32[]{:S(2)}) collective-permute-start(bf16[8,3584]{1,0:T(8,128)(2,1)S(1)} %collective-permute-done.2.refs_2_), channel_id=1, source_target_pairs={{0,1},{1,0},{2,3},{3,2},{4,5},{5,4},{6,7},{7,6},{8,9},{9,8},{10,11... | collective-permute-start | bytes 172040 | tf_op jit(solution)/shard_map/ppermute | solution.py:28
  13.3 4.3 %shard_map.73 = (bf16[3584,512]{1,0:T(8,128)(2,1)S(1)}, bf16[3584,512]{1,0:T(8,128)(2,1)S(1)}, bf16[512,3584]{1,0:T(8,128)(2,1)S(1)}) custom-call(bf16[3584,512]{1,0:T(8,128)(2,1)} %bitcast.21, bf16[3584,512]{1,0:T(8,128)(2,1)} %bitcast.22, bf16[512,3584]{1,0:T(8,128)(2,1)} %bitcast.23), custom_call_target="tpu_custom_call" | custom-call | tf_op jit(solution)/shard_map/pallas_call | solution.py:50
  17.7 2.3 %experts.2 = (bf16[32,3584]{1,0:T(8,128)(2,1)S(1)}, bf16[32,3584]{1,0:T(8,128)(2,1)S(1)}) custom-call(bf16[8,3584]{1,0:T(8,128)(2,1)S(1)} %bitcast.17, bf16[8,3584]{1,0:T(8,128)(2,1)S(1)} %collective-permute-done.1.refs_1_, bf16[8,3584]{1,0:T(8,128)(2,1)S(1)} %collective-permute-done.2.refs_2_, bf16[8,3584]{1,0:T(8,128)(2,1)S(1)} %collective-permute-done.3.refs_3_, ...), custom_call_target="tpu_custom_call" | custom-call | tf_op jit(solution)/shard_map/experts/pallas_call | solution.py:179
  21.8 1.8 %collective-permute-start.9 = (bf16[32,3584]{1,0:T(8,128)(2,1)S(1)}, bf16[32,3584]{1,0:T(8,128)(2,1)S(1)}, u32[]{:S(2)}, u32[]{:S(2)}) collective-permute-start(bf16[32,3584]{1,0:T(8,128)(2,1)S(1)} %get-tuple-element.24), channel_id=1, source_target_pairs={{0,9},{1,8},{2,11},{3,10},{4,13},{5,12},{6,15},{7,14},{8,17},{9,16... | collective-permute-start | bytes 688136 | tf_op jit(solution)/shard_map/ppermute | solution.py:28
  24.2 5.4 %collective-permute-done.8.refs_0_ = bf16[32,3584]{1,0:T(8,128)(2,1)S(1)} collective-permute-done((bf16[32,3584]{1,0:T(8,128)(2,1)S(1)}, bf16[32,3584]{1,0:T(8,128)(2,1)S(1)}, u32[]{:S(2)}, u32[]{:S(2)}) %collective-permute-start.8) | collective-permute-done | bytes 229408 | tf_op jit(solution)/shard_map/ppermute | solution.py:28
  29.9 2.4 %collective-permute-start.11 = (bf16[8,3584]{1,0:T(8,128)(2,1)S(1)}, bf16[8,3584]{1,0:T(8,128)(2,1)S(1)}, u32[]{:S(2)}, u32[]{:S(2)}) collective-permute-start(bf16[8,3584]{1,0:T(8,128)(2,1)S(1)} %get-tuple-element.27), channel_id=1, source_target_pairs={{0,4},{1,5},{2,6},{3,7},{4,0},{5,1},{6,2},{7,3},{8,12},{9,13},{10,... | collective-permute-start | bytes 172040 | tf_op jit(solution)/shard_map/ppermute | solution.py:28
  32.3 2.0 %collective-permute-start.12 = (bf16[8,3584]{1,0:T(8,128)(2,1)S(1)}, bf16[8,3584]{1,0:T(8,128)(2,1)S(1)}, u32[]{:S(2)}, u32[]{:S(2)}) collective-permute-start(bf16[8,3584]{1,0:T(8,128)(2,1)S(1)} %get-tuple-element.28), channel_id=1, source_target_pairs={{0,6},{1,7},{2,4},{3,5},{4,2},{5,3},{6,0},{7,1},{8,14},{9,15},{10,... | collective-permute-start | bytes 172040 | tf_op jit(solution)/shard_map/ppermute | solution.py:28
  35.5 2.0 %collective-permute-done.11.refs_2_ = bf16[8,3584]{1,0:T(8,128)(2,1)S(1)} collective-permute-done((bf16[8,3584]{1,0:T(8,128)(2,1)S(1)}, bf16[8,3584]{1,0:T(8,128)(2,1)S(1)}, u32[]{:S(2)}, u32[]{:S(2)}) %collective-permute-start.11) | collective-permute-done | bytes 57376 | tf_op jit(solution)/shard_map/ppermute | solution.py:28
  38.4 1.5 %collective-permute-start.14 = (bf16[8,3584]{1,0:T(8,128)(2,1)S(1)}, bf16[8,3584]{1,0:T(8,128)(2,1)S(1)}, u32[]{:S(2)}, u32[]{:S(2)}) collective-permute-start(bf16[8,3584]{1,0:T(8,128)(2,1)S(1)} %finish.2.own_ref.refs_0_), channel_id=1, source_target_pairs={{0,2},{1,3},{2,0},{3,1},{4,6},{5,7},{6,4},{7,5},{8,10},{9,11},{10,... | collective-permute-start | bytes 172040 | tf_op jit(solution)/shard_map/ppermute | solution.py:28
  41.2 1.6 %collective-permute-start.16 = (bf16[8,3584]{1,0:T(8,128)(2,1)S(1)}, bf16[8,3584]{1,0:T(8,128)(2,1)S(1)}, u32[]{:S(2)}, u32[]{:S(2)}) collective-permute-start(bf16[8,3584]{1,0:T(8,128)(2,1)S(1)} %finish.2.own_ref.refs_0_), channel_id=1, source_target_pairs={{0,6},{1,7},{2,4},{3,5},{4,2},{5,3},{6,0},{7,1},{8,14},{9,15},{10,... | collective-permute-start | bytes 172040 | tf_op jit(solution)/shard_map/ppermute | solution.py:28
  44.9 1.6 %collective-permute-done.15.refs_2_ = bf16[8,3584]{1,0:T(8,128)(2,1)S(1)} collective-permute-done((bf16[8,3584]{1,0:T(8,128)(2,1)S(1)}, bf16[8,3584]{1,0:T(8,128)(2,1)S(1)}, u32[]{:S(2)}, u32[]{:S(2)}) %collective-permute-start.15) | collective-permute-done | bytes 57376 | tf_op jit(solution)/shard_map/ppermute | solution.py:28
  49.1 1.6 %collective-permute-done.19.refs_6_ = bf16[8,3584]{1,0:T(8,128)(2,1)S(1)} collective-permute-done((bf16[8,3584]{1,0:T(8,128)(2,1)S(1)}, bf16[8,3584]{1,0:T(8,128)(2,1)S(1)}, u32[]{:S(2)}, u32[]{:S(2)}) %collective-permute-start.19) | collective-permute-done | bytes 57376 | tf_op jit(solution)/shard_map/ppermute | solution.py:28
  51.7 2.0 %copy-done.1 = bf16[3584,512]{1,0:T(8,128)(2,1)S(1)} copy-done((bf16[3584,512]{1,0:T(8,128)(2,1)S(1)}, bf16[3584,512]{1,0:T(8,128)(2,1)}, u32[]{:S(2)}) %copy-start.1) | copy-done | bytes 3670040
  53.8 2.0 %copy-done.3 = bf16[3584,512]{1,0:T(8,128)(2,1)S(1)} copy-done((bf16[3584,512]{1,0:T(8,128)(2,1)S(1)}, bf16[3584,512]{1,0:T(8,128)(2,1)}, u32[]{:S(2)}) %copy-start.3) | copy-done | bytes 3670040
  55.8 2.0 %copy-done.5 = bf16[512,3584]{1,0:T(8,128)(2,1)S(1)} copy-done((bf16[512,3584]{1,0:T(8,128)(2,1)S(1)}, bf16[512,3584]{1,0:T(8,128)(2,1)}, u32[]{:S(2)}) %copy-start.5) | copy-done | bytes 3670040
  57.8 2.2 %experts.3 = (bf16[32,3584]{1,0:T(8,128)(2,1)S(1)}, bf16[32,3584]{1,0:T(8,128)(2,1)S(1)}) custom-call(bf16[8,3584]{1,0:T(8,128)(2,1)S(1)} %finish.2.own_ref.refs_0_, bf16[8,3584]{1,0:T(8,128)(2,1)S(1)} %collective-permute-done.14.refs_1_, bf16[8,3584]{1,0:T(8,128)(2,1)S(1)} %collective-permute-done.15.refs_2_, ...), custom_call_target="tpu_custom_call" | custom-call | tf_op jit(solution)/shard_map/experts/pallas_call | solution.py:179
  62.2 5.6 %collective-permute-done.21.refs_0_ = bf16[32,3584]{1,0:T(8,128)(2,1)S(1)} collective-permute-done((bf16[32,3584]{1,0:T(8,128)(2,1)S(1)}, bf16[32,3584]{1,0:T(8,128)(2,1)S(1)}, u32[]{:S(2)}, u32[]{:S(2)}) %collective-permute-start.21) | collective-permute-done | bytes 229408 | tf_op jit(solution)/shard_map/ppermute | solution.py:28
  69.0 2.8 %collective-permute-start.24 = (bf16[8,3584]{1,0:T(8,128)(2,1)S(1)}, bf16[8,3584]{1,0:T(8,128)(2,1)S(1)}, u32[]{:S(2)}, u32[]{:S(2)}) collective-permute-start(bf16[8,3584]{1,0:T(8,128)(2,1)S(1)} %get-tuple-element.33), channel_id=1, source_target_pairs={{0,4},{1,5},{2,6},{3,7},{4,0},{5,1},{6,2},{7,3},{8,12},{9,13},{10,... | collective-permute-start | bytes 172040 | tf_op jit(solution)/shard_map/ppermute | solution.py:28
  73.2 2.9 %collective-permute-done.24.refs_2_ = bf16[8,3584]{1,0:T(8,128)(2,1)S(1)} collective-permute-done((bf16[8,3584]{1,0:T(8,128)(2,1)S(1)}, bf16[8,3584]{1,0:T(8,128)(2,1)S(1)}, u32[]{:S(2)}, u32[]{:S(2)}) %collective-permute-start.24) | collective-permute-done | bytes 57376 | tf_op jit(solution)/shard_map/ppermute | solution.py:28
  76.1 1.6 %collective-permute-done.25.refs_3_ = bf16[8,3584]{1,0:T(8,128)(2,1)S(1)} collective-permute-done((bf16[8,3584]{1,0:T(8,128)(2,1)S(1)}, bf16[8,3584]{1,0:T(8,128)(2,1)S(1)}, u32[]{:S(2)}, u32[]{:S(2)}) %collective-permute-start.25) | collective-permute-done | bytes 57376 | tf_op jit(solution)/shard_map/ppermute | solution.py:28
  (60 shorter events, 20.0 us)
Async XLA Ops:
  0.0 7.4 %collective-permute-start.1 = (bf16[8,3584]{1,0:T(8,128)(2,1)}, bf16[8,3584]{1,0:T(8,128)(2,1)S(1)}, u32[]{:S(2)}, u32[]{:S(2)}) collective-permute-start(bf16[8,3584]{1,0:T(8,128)(2,1)} %bitcast.13), channel_id=1, source_target_pairs={{0,2},{1,3},{2,0},{3,1},{4,6},{5,7},{6,4},{7,5},{8,10},{9,11},{10,... | collective-permute-start | bytes 172040 | tf_op jit(solution)/shard_map/ppermute | solution.py:28
  3.1 6.4 %collective-permute-start.2 = (bf16[8,3584]{1,0:T(8,128)(2,1)}, bf16[8,3584]{1,0:T(8,128)(2,1)S(1)}, u32[]{:S(2)}, u32[]{:S(2)}) collective-permute-start(bf16[8,3584]{1,0:T(8,128)(2,1)} %bitcast.14), channel_id=1, source_target_pairs={{0,4},{1,5},{2,6},{3,7},{4,0},{5,1},{6,2},{7,3},{8,12},{9,13},{10,... | collective-permute-start | bytes 172040 | tf_op jit(solution)/shard_map/ppermute | solution.py:28
  5.6 6.2 %collective-permute-start.3 = (bf16[8,3584]{1,0:T(8,128)(2,1)}, bf16[8,3584]{1,0:T(8,128)(2,1)S(1)}, u32[]{:S(2)}, u32[]{:S(2)}) collective-permute-start(bf16[8,3584]{1,0:T(8,128)(2,1)} %bitcast.15), channel_id=1, source_target_pairs={{0,6},{1,7},{2,4},{3,5},{4,2},{5,3},{6,0},{7,1},{8,14},{9,15},{10,... | collective-permute-start | bytes 172040 | tf_op jit(solution)/shard_map/ppermute | solution.py:28
  5.6 12.0 %collective-permute-start.4 = (bf16[8,3584]{1,0:T(8,128)(2,1)}, bf16[8,3584]{1,0:T(8,128)(2,1)S(1)}, u32[]{:S(2)}, u32[]{:S(2)}) collective-permute-start(bf16[8,3584]{1,0:T(8,128)(2,1)} %bitcast.16), channel_id=1, source_target_pairs={{0,1},{1,0},{2,3},{3,2},{4,5},{5,4},{6,7},{7,6},{8,9},{9,8},{10,11... | collective-permute-start | bytes 172040 | tf_op jit(solution)/shard_map/ppermute | solution.py:28
  7.4 10.3 %collective-permute-start.5 = (bf16[8,3584]{1,0:T(8,128)(2,1)S(1)}, bf16[8,3584]{1,0:T(8,128)(2,1)S(1)}, u32[]{:S(2)}, u32[]{:S(2)}) collective-permute-start(bf16[8,3584]{1,0:T(8,128)(2,1)S(1)} %collective-permute-done.1.refs_1_), channel_id=1, source_target_pairs={{0,1},{1,0},{2,3},{3,2},{4,5},{5,4},{6,7},{7,6},{8,9},{9,8},{10,11... | collective-permute-start | bytes 172040 | tf_op jit(solution)/shard_map/ppermute | solution.py:28
  9.5 8.2 %collective-permute-start.6 = (bf16[8,3584]{1,0:T(8,128)(2,1)S(1)}, bf16[8,3584]{1,0:T(8,128)(2,1)S(1)}, u32[]{:S(2)}, u32[]{:S(2)}) collective-permute-start(bf16[8,3584]{1,0:T(8,128)(2,1)S(1)} %collective-permute-done.2.refs_2_), channel_id=1, source_target_pairs={{0,1},{1,0},{2,3},{3,2},{4,5},{5,4},{6,7},{7,6},{8,9},{9,8},{10,11... | collective-permute-start | bytes 172040 | tf_op jit(solution)/shard_map/ppermute | solution.py:28
  11.8 5.8 %collective-permute-start.7 = (bf16[8,3584]{1,0:T(8,128)(2,1)S(1)}, bf16[8,3584]{1,0:T(8,128)(2,1)S(1)}, u32[]{:S(2)}, u32[]{:S(2)}) collective-permute-start(bf16[8,3584]{1,0:T(8,128)(2,1)S(1)} %collective-permute-done.3.refs_3_), channel_id=1, source_target_pairs={{0,1},{1,0},{2,3},{3,2},{4,5},{5,4},{6,7},{7,6},{8,9},{9,8},{10,11... | collective-permute-start | bytes 172040 | tf_op jit(solution)/shard_map/ppermute | solution.py:28
  21.8 7.8 %collective-permute-start.8 = (bf16[32,3584]{1,0:T(8,128)(2,1)S(1)}, bf16[32,3584]{1,0:T(8,128)(2,1)S(1)}, u32[]{:S(2)}, u32[]{:S(2)}) collective-permute-start(bf16[32,3584]{1,0:T(8,128)(2,1)S(1)} %get-tuple-element.23), channel_id=1, source_target_pairs={{0,8},{1,9},{2,10},{3,11},{4,12},{5,13},{6,14},{7,15},{8,16},{9,17... | collective-permute-start | bytes 688136 | tf_op jit(solution)/shard_map/ppermute | solution.py:28
  21.8 8.0 %collective-permute-start.9 = (bf16[32,3584]{1,0:T(8,128)(2,1)S(1)}, bf16[32,3584]{1,0:T(8,128)(2,1)S(1)}, u32[]{:S(2)}, u32[]{:S(2)}) collective-permute-start(bf16[32,3584]{1,0:T(8,128)(2,1)S(1)} %get-tuple-element.24), channel_id=1, source_target_pairs={{0,9},{1,8},{2,11},{3,10},{4,13},{5,12},{6,15},{7,14},{8,17},{9,16... | collective-permute-start | bytes 688136 | tf_op jit(solution)/shard_map/ppermute | solution.py:28
  24.1 10.1 %collective-permute-start = (bf16[8,3712]{1,0:T(8,128)(2,1)S(1)}, bf16[8,3712]{1,0:T(8,128)(2,1)S(1)}, u32[]{:S(2)}, u32[]{:S(2)}) collective-permute-start(bf16[8,3712]{1,0:T(8,128)(2,1)S(1)} %shares.2), channel_id=1, source_target_pairs={{0,8},{1,9},{2,10},{3,11},{4,12},{5,13},{6,14},{7,15},{8,16},{9,17... | collective-permute-start | bytes 178184 | tf_op jit(solution)/shard_map/ppermute | solution.py:28
  29.8 5.7 %collective-permute-start.10 = (bf16[8,3584]{1,0:T(8,128)(2,1)S(1)}, bf16[8,3584]{1,0:T(8,128)(2,1)S(1)}, u32[]{:S(2)}, u32[]{:S(2)}) collective-permute-start(bf16[8,3584]{1,0:T(8,128)(2,1)S(1)} %get-tuple-element.26), channel_id=1, source_target_pairs={{0,2},{1,3},{2,0},{3,1},{4,6},{5,7},{6,4},{7,5},{8,10},{9,11},{10,... | collective-permute-start | bytes 172040 | tf_op jit(solution)/shard_map/ppermute | solution.py:28
  29.9 7.6 %collective-permute-start.11 = (bf16[8,3584]{1,0:T(8,128)(2,1)S(1)}, bf16[8,3584]{1,0:T(8,128)(2,1)S(1)}, u32[]{:S(2)}, u32[]{:S(2)}) collective-permute-start(bf16[8,3584]{1,0:T(8,128)(2,1)S(1)} %get-tuple-element.27), channel_id=1, source_target_pairs={{0,4},{1,5},{2,6},{3,7},{4,0},{5,1},{6,2},{7,3},{8,12},{9,13},{10,... | collective-permute-start | bytes 172040 | tf_op jit(solution)/shard_map/ppermute | solution.py:28
  32.3 6.0 %collective-permute-start.12 = (bf16[8,3584]{1,0:T(8,128)(2,1)S(1)}, bf16[8,3584]{1,0:T(8,128)(2,1)S(1)}, u32[]{:S(2)}, u32[]{:S(2)}) collective-permute-start(bf16[8,3584]{1,0:T(8,128)(2,1)S(1)} %get-tuple-element.28), channel_id=1, source_target_pairs={{0,6},{1,7},{2,4},{3,5},{4,2},{5,3},{6,0},{7,1},{8,14},{9,15},{10,... | collective-permute-start | bytes 172040 | tf_op jit(solution)/shard_map/ppermute | solution.py:28
  38.4 5.9 %collective-permute-start.14 = (bf16[8,3584]{1,0:T(8,128)(2,1)S(1)}, bf16[8,3584]{1,0:T(8,128)(2,1)S(1)}, u32[]{:S(2)}, u32[]{:S(2)}) collective-permute-start(bf16[8,3584]{1,0:T(8,128)(2,1)S(1)} %finish.2.own_ref.refs_0_), channel_id=1, source_target_pairs={{0,2},{1,3},{2,0},{3,1},{4,6},{5,7},{6,4},{7,5},{8,10},{9,11},{10,... | collective-permute-start | bytes 172040 | tf_op jit(solution)/shard_map/ppermute | solution.py:28
  39.9 6.6 %collective-permute-start.15 = (bf16[8,3584]{1,0:T(8,128)(2,1)S(1)}, bf16[8,3584]{1,0:T(8,128)(2,1)S(1)}, u32[]{:S(2)}, u32[]{:S(2)}) collective-permute-start(bf16[8,3584]{1,0:T(8,128)(2,1)S(1)} %finish.2.own_ref.refs_0_), channel_id=1, source_target_pairs={{0,4},{1,5},{2,6},{3,7},{4,0},{5,1},{6,2},{7,3},{8,12},{9,13},{10,... | collective-permute-start | bytes 172040 | tf_op jit(solution)/shard_map/ppermute | solution.py:28
  41.2 6.3 %collective-permute-start.16 = (bf16[8,3584]{1,0:T(8,128)(2,1)S(1)}, bf16[8,3584]{1,0:T(8,128)(2,1)S(1)}, u32[]{:S(2)}, u32[]{:S(2)}) collective-permute-start(bf16[8,3584]{1,0:T(8,128)(2,1)S(1)} %finish.2.own_ref.refs_0_), channel_id=1, source_target_pairs={{0,6},{1,7},{2,4},{3,5},{4,2},{5,3},{6,0},{7,1},{8,14},{9,15},{10,... | collective-permute-start | bytes 172040 | tf_op jit(solution)/shard_map/ppermute | solution.py:28
  42.8 5.6 %collective-permute-start.17 = (bf16[8,3584]{1,0:T(8,128)(2,1)S(1)}, bf16[8,3584]{1,0:T(8,128)(2,1)S(1)}, u32[]{:S(2)}, u32[]{:S(2)}) collective-permute-start(bf16[8,3584]{1,0:T(8,128)(2,1)S(1)} %finish.2.own_ref.refs_0_), channel_id=1, source_target_pairs={{0,1},{1,0},{2,3},{3,2},{4,5},{5,4},{6,7},{7,6},{8,9},{9,8},{10,11... | collective-permute-start | bytes 172040 | tf_op jit(solution)/shard_map/ppermute | solution.py:28
  44.3 4.8 %collective-permute-start.18 = (bf16[8,3584]{1,0:T(8,128)(2,1)S(1)}, bf16[8,3584]{1,0:T(8,128)(2,1)S(1)}, u32[]{:S(2)}, u32[]{:S(2)}) collective-permute-start(bf16[8,3584]{1,0:T(8,128)(2,1)S(1)} %collective-permute-done.14.refs_1_), channel_id=1, source_target_pairs={{0,1},{1,0},{2,3},{3,2},{4,5},{5,4},{6,7},{7,6},{8,9},{9,8},{10,11... | collective-permute-start | bytes 172040 | tf_op jit(solution)/shard_map/ppermute | solution.py:28
  60.1 7.8 %collective-permute-start.21 = (bf16[32,3584]{1,0:T(8,128)(2,1)S(1)}, bf16[32,3584]{1,0:T(8,128)(2,1)S(1)}, u32[]{:S(2)}, u32[]{:S(2)}) collective-permute-start(bf16[32,3584]{1,0:T(8,128)(2,1)S(1)} %get-tuple-element.29), channel_id=1, source_target_pairs={{0,8},{1,9},{2,10},{3,11},{4,12},{5,13},{6,14},{7,15},{8,16},{9,17... | collective-permute-start | bytes 688136 | tf_op jit(solution)/shard_map/ppermute | solution.py:28
  60.1 8.1 %collective-permute-start.22 = (bf16[32,3584]{1,0:T(8,128)(2,1)S(1)}, bf16[32,3584]{1,0:T(8,128)(2,1)S(1)}, u32[]{:S(2)}, u32[]{:S(2)}) collective-permute-start(bf16[32,3584]{1,0:T(8,128)(2,1)S(1)} %get-tuple-element.30), channel_id=1, source_target_pairs={{0,9},{1,8},{2,11},{3,10},{4,13},{5,12},{6,15},{7,14},{8,17},{9,16... | collective-permute-start | bytes 688136 | tf_op jit(solution)/shard_map/ppermute | solution.py:28
  62.1 10.6 %collective-permute-start.13 = (bf16[8,3712]{1,0:T(8,128)(2,1)S(1)}, bf16[8,3712]{1,0:T(8,128)(2,1)S(1)}, u32[]{:S(2)}, u32[]{:S(2)}) collective-permute-start(bf16[8,3712]{1,0:T(8,128)(2,1)S(1)} %shares.3), channel_id=1, source_target_pairs={{0,8},{1,9},{2,10},{3,11},{4,12},{5,13},{6,14},{7,15},{8,16},{9,17... | collective-permute-start | bytes 178184 | tf_op jit(solution)/shard_map/ppermute | solution.py:28
  68.3 5.0 %collective-permute-start.23 = (bf16[8,3584]{1,0:T(8,128)(2,1)S(1)}, bf16[8,3584]{1,0:T(8,128)(2,1)S(1)}, u32[]{:S(2)}, u32[]{:S(2)}) collective-permute-start(bf16[8,3584]{1,0:T(8,128)(2,1)S(1)} %get-tuple-element.32), channel_id=1, source_target_pairs={{0,2},{1,3},{2,0},{3,1},{4,6},{5,7},{6,4},{7,5},{8,10},{9,11},{10,... | collective-permute-start | bytes 172040 | tf_op jit(solution)/shard_map/ppermute | solution.py:28
  69.0 7.1 %collective-permute-start.24 = (bf16[8,3584]{1,0:T(8,128)(2,1)S(1)}, bf16[8,3584]{1,0:T(8,128)(2,1)S(1)}, u32[]{:S(2)}, u32[]{:S(2)}) collective-permute-start(bf16[8,3584]{1,0:T(8,128)(2,1)S(1)} %get-tuple-element.33), channel_id=1, source_target_pairs={{0,4},{1,5},{2,6},{3,7},{4,0},{5,1},{6,2},{7,3},{8,12},{9,13},{10,... | collective-permute-start | bytes 172040 | tf_op jit(solution)/shard_map/ppermute | solution.py:28
  71.8 6.0 %collective-permute-start.25 = (bf16[8,3584]{1,0:T(8,128)(2,1)S(1)}, bf16[8,3584]{1,0:T(8,128)(2,1)S(1)}, u32[]{:S(2)}, u32[]{:S(2)}) collective-permute-start(bf16[8,3584]{1,0:T(8,128)(2,1)S(1)} %get-tuple-element.34), channel_id=1, source_target_pairs={{0,6},{1,7},{2,4},{3,5},{4,2},{5,3},{6,0},{7,1},{8,14},{9,15},{10,... | collective-permute-start | bytes 172040 | tf_op jit(solution)/shard_map/ppermute | solution.py:28
  (12 other events, 44.4 us)
where the time goes:
time: 78.7 us; the launch traced here: 78.5 us
  starting transfers between devices  31.5 us (40%)
  waiting for transfers between devices  28.1 us (36%)
  Pallas kernels  10.7 us (14%)
  local copies, waits for them, and re-layouts  8.09 us (10%)
    ppermute x26, starting transfers between devices, relayed(): return lax.ppermute(value, AXES, pairs)  31.5 us
    ppermute x26, waiting for transfers between devices, relayed(): return lax.ppermute(value, AXES, pairs)  28.1 us
    unnamed x20, local copies, waits for them, and re-layouts  7.93 us
    pallas_call x2, Pallas kernels, expert_parts(): pl.pallas_call(functools.partial(expert_kernel, count, shards), out_shape...  4.5 us
    pallas_call x1, Pallas kernels, fetched(): pl.pallas_call(functools.partial(fetch_kernel, count), out_shape=tuple((p...  4.26 us
  transfers between devices with their start and end apart: 26, of which 16 were waited for; matrix products, arithmetic and copies ran while one was open for 0% of the time, Pallas kernels for 7%

commit v1 on v0

--- a/solution.py
+++ b/solution.py
@@ -44,16 +44,17 @@
         copy.wait()
 
 
-def fetched(*weights):
+def fetched(weights, held=()):
     count = len(weights)
-    held = sum(w.size * w.dtype.itemsize for w in weights)
+    taken = sum(w.size * w.dtype.itemsize for w in (*weights, *held))
+    spare = min(w.size * w.dtype.itemsize for w in weights) * 4 // 5
     return pl.pallas_call(
         functools.partial(fetch_kernel, count),
         out_shape=tuple(pltpu.VMEM(w.shape, w.dtype) for w in weights),
         in_specs=[pl.BlockSpec(memory_space=pl.ANY)] * count,
         out_specs=[pl.BlockSpec(memory_space=pltpu.VMEM)] * count,
         scratch_shapes=[pltpu.SemaphoreType.DMA((count * FETCHES,))],
-        compiler_params=pltpu.CompilerParams(vmem_limit_bytes=VMEM_BYTES - held - held // 5),
+        compiler_params=pltpu.CompilerParams(vmem_limit_bytes=VMEM_BYTES - taken - spare),
     )(*weights)
 
 
@@ -209,16 +210,24 @@
 
     current = states[0]
     home = (lax.axis_index("expert") // shards).astype(jnp.int32)[None]
+    matrices = (w_gate[0], w_up[0], w_down[0])
     for tick in range(TICKS):
         blocks = gathered(current)
-        weights = fetched(w_gate[0], w_up[0], w_down[0])
+        if tick == 0:
+            early = fetched(matrices[:1])
+            weights = (*early, *fetched(matrices[1:], matrices[:1]))
+        parts = expert_parts(blocks, norm_gain, *weights, shards)
+        arrived = []
+        for j, part in enumerate(parts):
+            arrived.append(send(part, hop=1, expert_bits=0, shard_bits=j))
         shared = with_shares(current, routes[tick, 0], home, norm_gain, router[0].T)
         shared = send(shared, hop=1, expert_bits=0, shard_bits=0)
-        parts = expert_parts(blocks, norm_gain, *weights, shards)
-        sums = folded([send(part, hop=1, expert_bits=0, shard_bits=j) for j, part in enumerate(parts)], experts)
+        sums = folded(arrived, experts)
         pieces = {0: sums[0]}
         for k in far_first:
             pieces[k] = send(sums[k], hop=0, expert_bits=k, shard_bits=0)
+        if tick + 1 < TICKS:
+            weights = fetched(matrices)
         current = finished(shared, [pieces[k] for k in range(experts)])
     return current[None]
 

time: 78.7 us -> 72.6 us (0.922)
  local copies, waits for them, and re-layouts: 8.09 us -> 0.19 us
  Pallas kernels: 10.7 us -> 15.9 us
  waiting for transfers between devices: 28.1 us -> 24.1 us
    unnamed x20 -> x8, local copies, waits for them, and re-layouts: 7.93 us -> 0.03 us
    pallas_call x1 -> x3, Pallas kernels: 4.26 us -> 9.47 us  [fetched(): pl.pallas_call(functools.partial(fetch_kernel, count), out_shape=tuple((p...]
    ppermute x26, waiting for transfers between devices: 28.1 us -> 24.1 us  [relayed(): return lax.ppermute(value, AXES, pairs)]
  transfers between devices with their start and end apart: 26 -> 26, of which waited for: 16 -> 13; matrix products, arithmetic and copies ran while one was open for 0% -> 0% of each run, Pallas kernels for 7% -> 15%
where the time goes in v1:
time: 72.6 us; the launch traced here: 72.4 us
  starting transfers between devices  32 us (44%)
  waiting for transfers between devices  24.1 us (33%)
  Pallas kernels  15.9 us (22%)
    ppermute x26, starting transfers between devices, relayed(): return lax.ppermute(value, AXES, pairs)  32 us
    ppermute x26, waiting for transfers between devices, relayed(): return lax.ppermute(value, AXES, pairs)  24.1 us
    pallas_call x3, Pallas kernels, fetched(): pl.pallas_call(functools.partial(fetch_kernel, count), out_shape=tuple((p...  9.47 us
    pallas_call x2, Pallas kernels, expert_parts(): pl.pallas_call(functools.partial(expert_kernel, count, shards), out_shape...  4.49 us
  transfers between devices with their start and end apart: 26, of which 13 were waited for; matrix products, arithmetic and copies ran while one was open for 0% of the time, Pallas kernels for 15%

profile of v1, /device:TPU:0, one launch (start us, length us, event | category | flops | bytes accessed | tf_op | source)
XLA Modules:
  0.0 72.4 jit_solution(8611246375441845425)
XLA Ops:
  0.0 3.1 %collective-permute-start.1 = (bf16[8,3584]{1,0:T(8,128)(2,1)}, bf16[8,3584]{1,0:T(8,128)(2,1)S(1)}, u32[]{:S(2)}, u32[]{:S(2)}) collective-permute-start(bf16[8,3584]{1,0:T(8,128)(2,1)} %bitcast.13), channel_id=1, source_target_pairs={{0,2},{1,3},{2,0},{3,1},{4,6},{5,7},{6,4},{7,5},{8,10},{9,11},{10,... | collective-permute-start | bytes 172040 | tf_op jit(solution)/shard_map/ppermute | solution.py:28
  3.1 2.6 %collective-permute-start.2 = (bf16[8,3584]{1,0:T(8,128)(2,1)}, bf16[8,3584]{1,0:T(8,128)(2,1)S(1)}, u32[]{:S(2)}, u32[]{:S(2)}) collective-permute-start(bf16[8,3584]{1,0:T(8,128)(2,1)} %bitcast.14), channel_id=1, source_target_pairs={{0,4},{1,5},{2,6},{3,7},{4,0},{5,1},{6,2},{7,3},{8,12},{9,13},{10,... | collective-permute-start | bytes 172040 | tf_op jit(solution)/shard_map/ppermute | solution.py:28
  5.6 1.7 %collective-permute-start.4 = (bf16[8,3584]{1,0:T(8,128)(2,1)}, bf16[8,3584]{1,0:T(8,128)(2,1)S(1)}, u32[]{:S(2)}, u32[]{:S(2)}) collective-permute-start(bf16[8,3584]{1,0:T(8,128)(2,1)} %bitcast.16), channel_id=1, source_target_pairs={{0,1},{1,0},{2,3},{3,2},{4,5},{5,4},{6,7},{7,6},{8,9},{9,8},{10,11... | collective-permute-start | bytes 172040 | tf_op jit(solution)/shard_map/ppermute | solution.py:28
  7.7 1.8 %collective-permute-done.2.refs_2_ = bf16[8,3584]{1,0:T(8,128)(2,1)S(1)} collective-permute-done((bf16[8,3584]{1,0:T(8,128)(2,1)}, bf16[8,3584]{1,0:T(8,128)(2,1)S(1)}, u32[]{:S(2)}, u32[]{:S(2)}) %collective-permute-start.2) | collective-permute-done | bytes 57376 | tf_op jit(solution)/shard_map/ppermute | solution.py:28
  9.5 1.5 %collective-permute-start.6 = (bf16[8,3584]{1,0:T(8,128)(2,1)S(1)}, bf16[8,3584]{1,0:T(8,128)(2,1)S(1)}, u32[]{:S(2)}, u32[]{:S(2)}) collective-permute-start(bf16[8,3584]{1,0:T(8,128)(2,1)S(1)} %collective-permute-done.2.refs_2_), channel_id=1, source_target_pairs={{0,1},{1,0},{2,3},{3,2},{4,5},{5,4},{6,7},{7,6},{8,9},{9,8},{10,11... | collective-permute-start | bytes 172040 | tf_op jit(solution)/shard_map/ppermute | solution.py:28
  11.8 1.5 %collective-permute-start.7 = (bf16[8,3584]{1,0:T(8,128)(2,1)S(1)}, bf16[8,3584]{1,0:T(8,128)(2,1)S(1)}, u32[]{:S(2)}, u32[]{:S(2)}) collective-permute-start(bf16[8,3584]{1,0:T(8,128)(2,1)S(1)} %collective-permute-done.3.refs_3_), channel_id=1, source_target_pairs={{0,1},{1,0},{2,3},{3,2},{4,5},{5,4},{6,7},{7,6},{8,9},{9,8},{10,11... | collective-permute-start | bytes 172040 | tf_op jit(solution)/shard_map/ppermute | solution.py:28
  13.3 2.0 %shard_map.73.refs_9_ = bf16[3584,512]{1,0:T(8,128)(2,1)S(1)} custom-call(bf16[3584,512]{1,0:T(8,128)(2,1)} %bitcast.21), custom_call_target="tpu_custom_call" | custom-call | tf_op jit(solution)/shard_map/pallas_call | solution.py:51
  15.4 3.2 %shard_map.74 = (bf16[3584,512]{1,0:T(8,128)(2,1)S(1)}, bf16[512,3584]{1,0:T(8,128)(2,1)S(1)}) custom-call(bf16[3584,512]{1,0:T(8,128)(2,1)} %bitcast.23, bf16[512,3584]{1,0:T(8,128)(2,1)} %bitcast.25), custom_call_target="tpu_custom_call" | custom-call | tf_op jit(solution)/shard_map/pallas_call | solution.py:51
  18.7 2.2 %experts.2 = (bf16[32,3584]{1,0:T(8,128)(2,1)S(1)}, bf16[32,3584]{1,0:T(8,128)(2,1)S(1)}) custom-call(bf16[8,3584]{1,0:T(8,128)(2,1)S(1)} %bitcast.17, bf16[8,3584]{1,0:T(8,128)(2,1)S(1)} %collective-permute-done.1.refs_1_, bf16[8,3584]{1,0:T(8,128)(2,1)S(1)} %collective-permute-done.2.refs_2_, bf16[8,3584]{1,0:T(8,128)(2,1)S(1)} %collective-permute-done.3.refs_3_, ...), custom_call_target="tpu_custom_call" | custom-call | tf_op jit(solution)/shard_map/experts/pallas_call | solution.py:180
  21.0 1.8 %collective-permute-start.9 = (bf16[32,3584]{1,0:T(8,128)(2,1)S(1)}, bf16[32,3584]{1,0:T(8,128)(2,1)S(1)}, u32[]{:S(2)}, u32[]{:S(2)}) collective-permute-start(bf16[32,3584]{1,0:T(8,128)(2,1)S(1)} %get-tuple-element.25), channel_id=1, source_target_pairs={{0,9},{1,8},{2,11},{3,10},{4,13},{5,12},{6,15},{7,14},{8,17},{9,16... | collective-permute-start | bytes 688136 | tf_op jit(solution)/shard_map/ppermute | solution.py:28
  23.4 5.3 %collective-permute-done.8.refs_0_ = bf16[32,3584]{1,0:T(8,128)(2,1)S(1)} collective-permute-done((bf16[32,3584]{1,0:T(8,128)(2,1)S(1)}, bf16[32,3584]{1,0:T(8,128)(2,1)S(1)}, u32[]{:S(2)}, u32[]{:S(2)}) %collective-permute-start.8) | collective-permute-done | bytes 229408 | tf_op jit(solution)/shard_map/ppermute | solution.py:28
  29.2 2.3 %collective-permute-start.11 = (bf16[8,3584]{1,0:T(8,128)(2,1)S(1)}, bf16[8,3584]{1,0:T(8,128)(2,1)S(1)}, u32[]{:S(2)}, u32[]{:S(2)}) collective-permute-start(bf16[8,3584]{1,0:T(8,128)(2,1)S(1)} %get-tuple-element.28), channel_id=1, source_target_pairs={{0,4},{1,5},{2,6},{3,7},{4,0},{5,1},{6,2},{7,3},{8,12},{9,13},{10,... | collective-permute-start | bytes 172040 | tf_op jit(solution)/shard_map/ppermute | solution.py:28
  31.5 2.0 %collective-permute-start.12 = (bf16[8,3584]{1,0:T(8,128)(2,1)S(1)}, bf16[8,3584]{1,0:T(8,128)(2,1)S(1)}, u32[]{:S(2)}, u32[]{:S(2)}) collective-permute-start(bf16[8,3584]{1,0:T(8,128)(2,1)S(1)} %get-tuple-element.29), channel_id=1, source_target_pairs={{0,6},{1,7},{2,4},{3,5},{4,2},{5,3},{6,0},{7,1},{8,14},{9,15},{10,... | collective-permute-start | bytes 172040 | tf_op jit(solution)/shard_map/ppermute | solution.py:28
  34.7 2.1 %collective-permute-done.11.refs_2_ = bf16[8,3584]{1,0:T(8,128)(2,1)S(1)} collective-permute-done((bf16[8,3584]{1,0:T(8,128)(2,1)S(1)}, bf16[8,3584]{1,0:T(8,128)(2,1)S(1)}, u32[]{:S(2)}, u32[]{:S(2)}) %collective-permute-start.11) | collective-permute-done | bytes 57376 | tf_op jit(solution)/shard_map/ppermute | solution.py:28
  37.6 1.5 %collective-permute-start.14 = (bf16[8,3584]{1,0:T(8,128)(2,1)S(1)}, bf16[8,3584]{1,0:T(8,128)(2,1)S(1)}, u32[]{:S(2)}, u32[]{:S(2)}) collective-permute-start(bf16[8,3584]{1,0:T(8,128)(2,1)S(1)} %finish.2.own_ref.refs_0_), channel_id=1, source_target_pairs={{0,2},{1,3},{2,0},{3,1},{4,6},{5,7},{6,4},{7,5},{8,10},{9,11},{10,... | collective-permute-start | bytes 172040 | tf_op jit(solution)/shard_map/ppermute | solution.py:28
  40.5 1.6 %collective-permute-start.16 = (bf16[8,3584]{1,0:T(8,128)(2,1)S(1)}, bf16[8,3584]{1,0:T(8,128)(2,1)S(1)}, u32[]{:S(2)}, u32[]{:S(2)}) collective-permute-start(bf16[8,3584]{1,0:T(8,128)(2,1)S(1)} %finish.2.own_ref.refs_0_), channel_id=1, source_target_pairs={{0,6},{1,7},{2,4},{3,5},{4,2},{5,3},{6,0},{7,1},{8,14},{9,15},{10,... | collective-permute-start | bytes 172040 | tf_op jit(solution)/shard_map/ppermute | solution.py:28
  42.1 1.5 %collective-permute-start.17 = (bf16[8,3584]{1,0:T(8,128)(2,1)S(1)}, bf16[8,3584]{1,0:T(8,128)(2,1)S(1)}, u32[]{:S(2)}, u32[]{:S(2)}) collective-permute-start(bf16[8,3584]{1,0:T(8,128)(2,1)S(1)} %finish.2.own_ref.refs_0_), channel_id=1, source_target_pairs={{0,1},{1,0},{2,3},{3,2},{4,5},{5,4},{6,7},{7,6},{8,9},{9,8},{10,11... | collective-permute-start | bytes 172040 | tf_op jit(solution)/shard_map/ppermute | solution.py:28
  44.1 1.5 %collective-permute-done.15.refs_2_ = bf16[8,3584]{1,0:T(8,128)(2,1)S(1)} collective-permute-done((bf16[8,3584]{1,0:T(8,128)(2,1)S(1)}, bf16[8,3584]{1,0:T(8,128)(2,1)S(1)}, u32[]{:S(2)}, u32[]{:S(2)}) %collective-permute-start.15) | collective-permute-done | bytes 57376 | tf_op jit(solution)/shard_map/ppermute | solution.py:28
  47.6 4.2 %shard_map.75 = (bf16[3584,512]{1,0:T(8,128)(2,1)S(1)}, bf16[3584,512]{1,0:T(8,128)(2,1)S(1)}, bf16[512,3584]{1,0:T(8,128)(2,1)S(1)}) custom-call(bf16[3584,512]{1,0:T(8,128)(2,1)} %bitcast.22, bf16[3584,512]{1,0:T(8,128)(2,1)} %bitcast.24, bf16[512,3584]{1,0:T(8,128)(2,1)} %bitcast.26), custom_call_target="tpu_custom_call" | custom-call | tf_op jit(solution)/shard_map/pallas_call | solution.py:51
  51.9 2.2 %experts.3 = (bf16[32,3584]{1,0:T(8,128)(2,1)S(1)}, bf16[32,3584]{1,0:T(8,128)(2,1)S(1)}) custom-call(bf16[8,3584]{1,0:T(8,128)(2,1)S(1)} %finish.2.own_ref.refs_0_, bf16[8,3584]{1,0:T(8,128)(2,1)S(1)} %collective-permute-done.14.refs_1_, bf16[8,3584]{1,0:T(8,128)(2,1)S(1)} %collective-permute-done.15.refs_2_, ...), custom_call_target="tpu_custom_call" | custom-call | tf_op jit(solution)/shard_map/experts/pallas_call | solution.py:180
  54.3 2.0 %collective-permute-start.22 = (bf16[32,3584]{1,0:T(8,128)(2,1)S(1)}, bf16[32,3584]{1,0:T(8,128)(2,1)S(1)}, u32[]{:S(2)}, u32[]{:S(2)}) collective-permute-start(bf16[32,3584]{1,0:T(8,128)(2,1)S(1)} %get-tuple-element.34), channel_id=1, source_target_pairs={{0,9},{1,8},{2,11},{3,10},{4,13},{5,12},{6,15},{7,14},{8,17},{9,16... | collective-permute-start | bytes 688136 | tf_op jit(solution)/shard_map/ppermute | solution.py:28
  56.9 5.1 %collective-permute-done.21.refs_0_ = bf16[32,3584]{1,0:T(8,128)(2,1)S(1)} collective-permute-done((bf16[32,3584]{1,0:T(8,128)(2,1)S(1)}, bf16[32,3584]{1,0:T(8,128)(2,1)S(1)}, u32[]{:S(2)}, u32[]{:S(2)}) %collective-permute-start.21) | collective-permute-done | bytes 229408 | tf_op jit(solution)/shard_map/ppermute | solution.py:28
  63.3 2.3 %collective-permute-start.24 = (bf16[8,3584]{1,0:T(8,128)(2,1)S(1)}, bf16[8,3584]{1,0:T(8,128)(2,1)S(1)}, u32[]{:S(2)}, u32[]{:S(2)}) collective-permute-start(bf16[8,3584]{1,0:T(8,128)(2,1)S(1)} %get-tuple-element.37), channel_id=1, source_target_pairs={{0,4},{1,5},{2,6},{3,7},{4,0},{5,1},{6,2},{7,3},{8,12},{9,13},{10,... | collective-permute-start | bytes 172040 | tf_op jit(solution)/shard_map/ppermute | solution.py:28
  67.2 3.4 %collective-permute-done.24.refs_2_ = bf16[8,3584]{1,0:T(8,128)(2,1)S(1)} collective-permute-done((bf16[8,3584]{1,0:T(8,128)(2,1)S(1)}, bf16[8,3584]{1,0:T(8,128)(2,1)S(1)}, u32[]{:S(2)}, u32[]{:S(2)}) %collective-permute-start.24) | collective-permute-done | bytes 57376 | tf_op jit(solution)/shard_map/ppermute | solution.py:28
  (50 shorter events, 13.8 us)
Async XLA Ops:
  0.0 7.4 %collective-permute-start.1 = (bf16[8,3584]{1,0:T(8,128)(2,1)}, bf16[8,3584]{1,0:T(8,128)(2,1)S(1)}, u32[]{:S(2)}, u32[]{:S(2)}) collective-permute-start(bf16[8,3584]{1,0:T(8,128)(2,1)} %bitcast.13), channel_id=1, source_target_pairs={{0,2},{1,3},{2,0},{3,1},{4,6},{5,7},{6,4},{7,5},{8,10},{9,11},{10,... | collective-permute-start | bytes 172040 | tf_op jit(solution)/shard_map/ppermute | solution.py:28
  3.1 6.4 %collective-permute-start.2 = (bf16[8,3584]{1,0:T(8,128)(2,1)}, bf16[8,3584]{1,0:T(8,128)(2,1)S(1)}, u32[]{:S(2)}, u32[]{:S(2)}) collective-permute-start(bf16[8,3584]{1,0:T(8,128)(2,1)} %bitcast.14), channel_id=1, source_target_pairs={{0,4},{1,5},{2,6},{3,7},{4,0},{5,1},{6,2},{7,3},{8,12},{9,13},{10,... | collective-permute-start | bytes 172040 | tf_op jit(solution)/shard_map/ppermute | solution.py:28
  5.6 6.2 %collective-permute-start.3 = (bf16[8,3584]{1,0:T(8,128)(2,1)}, bf16[8,3584]{1,0:T(8,128)(2,1)S(1)}, u32[]{:S(2)}, u32[]{:S(2)}) collective-permute-start(bf16[8,3584]{1,0:T(8,128)(2,1)} %bitcast.15), channel_id=1, source_target_pairs={{0,6},{1,7},{2,4},{3,5},{4,2},{5,3},{6,0},{7,1},{8,14},{9,15},{10,... | collective-permute-start | bytes 172040 | tf_op jit(solution)/shard_map/ppermute | solution.py:28
  5.6 12.9 %collective-permute-start.4 = (bf16[8,3584]{1,0:T(8,128)(2,1)}, bf16[8,3584]{1,0:T(8,128)(2,1)S(1)}, u32[]{:S(2)}, u32[]{:S(2)}) collective-permute-start(bf16[8,3584]{1,0:T(8,128)(2,1)} %bitcast.16), channel_id=1, source_target_pairs={{0,1},{1,0},{2,3},{3,2},{4,5},{5,4},{6,7},{7,6},{8,9},{9,8},{10,11... | collective-permute-start | bytes 172040 | tf_op jit(solution)/shard_map/ppermute | solution.py:28
  7.4 11.2 %collective-permute-start.5 = (bf16[8,3584]{1,0:T(8,128)(2,1)S(1)}, bf16[8,3584]{1,0:T(8,128)(2,1)S(1)}, u32[]{:S(2)}, u32[]{:S(2)}) collective-permute-start(bf16[8,3584]{1,0:T(8,128)(2,1)S(1)} %collective-permute-done.1.refs_1_), channel_id=1, source_target_pairs={{0,1},{1,0},{2,3},{3,2},{4,5},{5,4},{6,7},{7,6},{8,9},{9,8},{10,11... | collective-permute-start | bytes 172040 | tf_op jit(solution)/shard_map/ppermute | solution.py:28
  9.5 9.2 %collective-permute-start.6 = (bf16[8,3584]{1,0:T(8,128)(2,1)S(1)}, bf16[8,3584]{1,0:T(8,128)(2,1)S(1)}, u32[]{:S(2)}, u32[]{:S(2)}) collective-permute-start(bf16[8,3584]{1,0:T(8,128)(2,1)S(1)} %collective-permute-done.2.refs_2_), channel_id=1, source_target_pairs={{0,1},{1,0},{2,3},{3,2},{4,5},{5,4},{6,7},{7,6},{8,9},{9,8},{10,11... | collective-permute-start | bytes 172040 | tf_op jit(solution)/shard_map/ppermute | solution.py:28
  11.8 6.8 %collective-permute-start.7 = (bf16[8,3584]{1,0:T(8,128)(2,1)S(1)}, bf16[8,3584]{1,0:T(8,128)(2,1)S(1)}, u32[]{:S(2)}, u32[]{:S(2)}) collective-permute-start(bf16[8,3584]{1,0:T(8,128)(2,1)S(1)} %collective-permute-done.3.refs_3_), channel_id=1, source_target_pairs={{0,1},{1,0},{2,3},{3,2},{4,5},{5,4},{6,7},{7,6},{8,9},{9,8},{10,11... | collective-permute-start | bytes 172040 | tf_op jit(solution)/shard_map/ppermute | solution.py:28
  20.9 7.8 %collective-permute-start.8 = (bf16[32,3584]{1,0:T(8,128)(2,1)S(1)}, bf16[32,3584]{1,0:T(8,128)(2,1)S(1)}, u32[]{:S(2)}, u32[]{:S(2)}) collective-permute-start(bf16[32,3584]{1,0:T(8,128)(2,1)S(1)} %get-tuple-element.24), channel_id=1, source_target_pairs={{0,8},{1,9},{2,10},{3,11},{4,12},{5,13},{6,14},{7,15},{8,16},{9,17... | collective-permute-start | bytes 688136 | tf_op jit(solution)/shard_map/ppermute | solution.py:28
  21.0 8.1 %collective-permute-start.9 = (bf16[32,3584]{1,0:T(8,128)(2,1)S(1)}, bf16[32,3584]{1,0:T(8,128)(2,1)S(1)}, u32[]{:S(2)}, u32[]{:S(2)}) collective-permute-start(bf16[32,3584]{1,0:T(8,128)(2,1)S(1)} %get-tuple-element.25), channel_id=1, source_target_pairs={{0,9},{1,8},{2,11},{3,10},{4,13},{5,12},{6,15},{7,14},{8,17},{9,16... | collective-permute-start | bytes 688136 | tf_op jit(solution)/shard_map/ppermute | solution.py:28
  23.3 10.2 %collective-permute-start = (bf16[8,3712]{1,0:T(8,128)(2,1)S(1)}, bf16[8,3712]{1,0:T(8,128)(2,1)S(1)}, u32[]{:S(2)}, u32[]{:S(2)}) collective-permute-start(bf16[8,3712]{1,0:T(8,128)(2,1)S(1)} %shares.2), channel_id=1, source_target_pairs={{0,8},{1,9},{2,10},{3,11},{4,12},{5,13},{6,14},{7,15},{8,16},{9,17... | collective-permute-start | bytes 178184 | tf_op jit(solution)/shard_map/ppermute | solution.py:28
  29.1 5.6 %collective-permute-start.10 = (bf16[8,3584]{1,0:T(8,128)(2,1)S(1)}, bf16[8,3584]{1,0:T(8,128)(2,1)S(1)}, u32[]{:S(2)}, u32[]{:S(2)}) collective-permute-start(bf16[8,3584]{1,0:T(8,128)(2,1)S(1)} %get-tuple-element.27), channel_id=1, source_target_pairs={{0,2},{1,3},{2,0},{3,1},{4,6},{5,7},{6,4},{7,5},{8,10},{9,11},{10,... | collective-permute-start | bytes 172040 | tf_op jit(solution)/shard_map/ppermute | solution.py:28
  29.2 7.6 %collective-permute-start.11 = (bf16[8,3584]{1,0:T(8,128)(2,1)S(1)}, bf16[8,3584]{1,0:T(8,128)(2,1)S(1)}, u32[]{:S(2)}, u32[]{:S(2)}) collective-permute-start(bf16[8,3584]{1,0:T(8,128)(2,1)S(1)} %get-tuple-element.28), channel_id=1, source_target_pairs={{0,4},{1,5},{2,6},{3,7},{4,0},{5,1},{6,2},{7,3},{8,12},{9,13},{10,... | collective-permute-start | bytes 172040 | tf_op jit(solution)/shard_map/ppermute | solution.py:28
  31.5 6.0 %collective-permute-start.12 = (bf16[8,3584]{1,0:T(8,128)(2,1)S(1)}, bf16[8,3584]{1,0:T(8,128)(2,1)S(1)}, u32[]{:S(2)}, u32[]{:S(2)}) collective-permute-start(bf16[8,3584]{1,0:T(8,128)(2,1)S(1)} %get-tuple-element.29), channel_id=1, source_target_pairs={{0,6},{1,7},{2,4},{3,5},{4,2},{5,3},{6,0},{7,1},{8,14},{9,15},{10,... | collective-permute-start | bytes 172040 | tf_op jit(solution)/shard_map/ppermute | solution.py:28
  37.6 6.0 %collective-permute-start.14 = (bf16[8,3584]{1,0:T(8,128)(2,1)S(1)}, bf16[8,3584]{1,0:T(8,128)(2,1)S(1)}, u32[]{:S(2)}, u32[]{:S(2)}) collective-permute-start(bf16[8,3584]{1,0:T(8,128)(2,1)S(1)} %finish.2.own_ref.refs_0_), channel_id=1, source_target_pairs={{0,2},{1,3},{2,0},{3,1},{4,6},{5,7},{6,4},{7,5},{8,10},{9,11},{10,... | collective-permute-start | bytes 172040 | tf_op jit(solution)/shard_map/ppermute | solution.py:28
  39.1 6.5 %collective-permute-start.15 = (bf16[8,3584]{1,0:T(8,128)(2,1)S(1)}, bf16[8,3584]{1,0:T(8,128)(2,1)S(1)}, u32[]{:S(2)}, u32[]{:S(2)}) collective-permute-start(bf16[8,3584]{1,0:T(8,128)(2,1)S(1)} %finish.2.own_ref.refs_0_), channel_id=1, source_target_pairs={{0,4},{1,5},{2,6},{3,7},{4,0},{5,1},{6,2},{7,3},{8,12},{9,13},{10,... | collective-permute-start | bytes 172040 | tf_op jit(solution)/shard_map/ppermute | solution.py:28
  40.5 6.2 %collective-permute-start.16 = (bf16[8,3584]{1,0:T(8,128)(2,1)S(1)}, bf16[8,3584]{1,0:T(8,128)(2,1)S(1)}, u32[]{:S(2)}, u32[]{:S(2)}) collective-permute-start(bf16[8,3584]{1,0:T(8,128)(2,1)S(1)} %finish.2.own_ref.refs_0_), channel_id=1, source_target_pairs={{0,6},{1,7},{2,4},{3,5},{4,2},{5,3},{6,0},{7,1},{8,14},{9,15},{10,... | collective-permute-start | bytes 172040 | tf_op jit(solution)/shard_map/ppermute | solution.py:28
  42.1 9.8 %collective-permute-start.17 = (bf16[8,3584]{1,0:T(8,128)(2,1)S(1)}, bf16[8,3584]{1,0:T(8,128)(2,1)S(1)}, u32[]{:S(2)}, u32[]{:S(2)}) collective-permute-start(bf16[8,3584]{1,0:T(8,128)(2,1)S(1)} %finish.2.own_ref.refs_0_), channel_id=1, source_target_pairs={{0,1},{1,0},{2,3},{3,2},{4,5},{5,4},{6,7},{7,6},{8,9},{9,8},{10,11... | collective-permute-start | bytes 172040 | tf_op jit(solution)/shard_map/ppermute | solution.py:28
  43.6 8.3 %collective-permute-start.18 = (bf16[8,3584]{1,0:T(8,128)(2,1)S(1)}, bf16[8,3584]{1,0:T(8,128)(2,1)S(1)}, u32[]{:S(2)}, u32[]{:S(2)}) collective-permute-start(bf16[8,3584]{1,0:T(8,128)(2,1)S(1)} %collective-permute-done.14.refs_1_), channel_id=1, source_target_pairs={{0,1},{1,0},{2,3},{3,2},{4,5},{5,4},{6,7},{7,6},{8,9},{9,8},{10,11... | collective-permute-start | bytes 172040 | tf_op jit(solution)/shard_map/ppermute | solution.py:28
  45.6 6.3 %collective-permute-start.19 = (bf16[8,3584]{1,0:T(8,128)(2,1)S(1)}, bf16[8,3584]{1,0:T(8,128)(2,1)S(1)}, u32[]{:S(2)}, u32[]{:S(2)}) collective-permute-start(bf16[8,3584]{1,0:T(8,128)(2,1)S(1)} %collective-permute-done.15.refs_2_), channel_id=1, source_target_pairs={{0,1},{1,0},{2,3},{3,2},{4,5},{5,4},{6,7},{7,6},{8,9},{9,8},{10,11... | collective-permute-start | bytes 172040 | tf_op jit(solution)/shard_map/ppermute | solution.py:28
  54.2 7.8 %collective-permute-start.21 = (bf16[32,3584]{1,0:T(8,128)(2,1)S(1)}, bf16[32,3584]{1,0:T(8,128)(2,1)S(1)}, u32[]{:S(2)}, u32[]{:S(2)}) collective-permute-start(bf16[32,3584]{1,0:T(8,128)(2,1)S(1)} %get-tuple-element.33), channel_id=1, source_target_pairs={{0,8},{1,9},{2,10},{3,11},{4,12},{5,13},{6,14},{7,15},{8,16},{9,17... | collective-permute-start | bytes 688136 | tf_op jit(solution)/shard_map/ppermute | solution.py:28
  54.3 8.1 %collective-permute-start.22 = (bf16[32,3584]{1,0:T(8,128)(2,1)S(1)}, bf16[32,3584]{1,0:T(8,128)(2,1)S(1)}, u32[]{:S(2)}, u32[]{:S(2)}) collective-permute-start(bf16[32,3584]{1,0:T(8,128)(2,1)S(1)} %get-tuple-element.34), channel_id=1, source_target_pairs={{0,9},{1,8},{2,11},{3,10},{4,13},{5,12},{6,15},{7,14},{8,17},{9,16... | collective-permute-start | bytes 688136 | tf_op jit(solution)/shard_map/ppermute | solution.py:28
  56.8 10.0 %collective-permute-start.13 = (bf16[8,3712]{1,0:T(8,128)(2,1)S(1)}, bf16[8,3712]{1,0:T(8,128)(2,1)S(1)}, u32[]{:S(2)}, u32[]{:S(2)}) collective-permute-start(bf16[8,3712]{1,0:T(8,128)(2,1)S(1)} %shares.3), channel_id=1, source_target_pairs={{0,8},{1,9},{2,10},{3,11},{4,12},{5,13},{6,14},{7,15},{8,16},{9,17... | collective-permute-start | bytes 178184 | tf_op jit(solution)/shard_map/ppermute | solution.py:28
  63.3 7.4 %collective-permute-start.24 = (bf16[8,3584]{1,0:T(8,128)(2,1)S(1)}, bf16[8,3584]{1,0:T(8,128)(2,1)S(1)}, u32[]{:S(2)}, u32[]{:S(2)}) collective-permute-start(bf16[8,3584]{1,0:T(8,128)(2,1)S(1)} %get-tuple-element.37), channel_id=1, source_target_pairs={{0,4},{1,5},{2,6},{3,7},{4,0},{5,1},{6,2},{7,3},{8,12},{9,13},{10,... | collective-permute-start | bytes 172040 | tf_op jit(solution)/shard_map/ppermute | solution.py:28
  65.6 6.1 %collective-permute-start.25 = (bf16[8,3584]{1,0:T(8,128)(2,1)S(1)}, bf16[8,3584]{1,0:T(8,128)(2,1)S(1)}, u32[]{:S(2)}, u32[]{:S(2)}) collective-permute-start(bf16[8,3584]{1,0:T(8,128)(2,1)S(1)} %get-tuple-element.38), channel_id=1, source_target_pairs={{0,6},{1,7},{2,4},{3,5},{4,2},{5,3},{6,0},{7,1},{8,14},{9,15},{10,... | collective-permute-start | bytes 172040 | tf_op jit(solution)/shard_map/ppermute | solution.py:28
  (6 other events, 24.9 us)
